TPU v7x, 256 devices: a whole 4x4x8 slice. The times are simulated.
256 devices in a mesh: freq: 64 (over y, z, core), sky: 4 (over x).
Axes of the slice: x: 4, y: 4, z: 8, core: 2. Of those that a mesh axis runs over, the one named last changes fastest.
Arguments:
- sky_maps: bfloat16 [1024, 96, 4096], P('freq', 'sky'), may hold values from -240 to 240
- beam_index: int32 [1024], P('freq'), may hold values from 0 to 7
- beam_taps: float32 [8, 31], replicated, may hold values from 0.05 to 1
- start_seed: int32 [1024, 16], replicated, may hold values from -64 to 64
Outputs:
- cleaned: bfloat16 [1024, 256, 1536], P(None, ('freq', 'sky'))
All inputs are finite; a program needn't handle non-finite values.
Results may differ from a plain program's by a relative error of at most 0.0079.
The roundings to bfloat16 on the way count: a program that leaves them out, or rounds other values in their place, can miss the bound.
Values may be sent and summed in bfloat16 or wider, within the bound.
No kernel may reach another device: no remote copies, remote signals or barrier semaphores. Data moves between devices by JAX's collectives and lax.ppermute only.
A program may use at most 64 MiB of HBM per device.

v0:
```python
import jax
import jax.numpy as jnp
from jax import lax
from jax.sharding import PartitionSpec as P

ITERS = 8


def with_halo(x, sides, width):
    for axis, dim in sides:
        size, length = (lax.axis_size(axis), x.shape[dim])
        up = [(i, (i + 1) % size) for i in range(size - 1)]
        down = [(j, i) for i, j in up]
        last = lax.slice_in_dim(x, length - width, length, axis=dim)
        leading = lax.slice_in_dim(x, 0, width, axis=dim)
        before = lax.ppermute(last, axis, up)
        after = lax.ppermute(leading, axis, down)
        x = jnp.concatenate([before, x, after], axis=dim)
    return x


def column_pass(padded, kernels, strip_rows, half_taps, tap_count):
    row_pass = jnp.zeros((padded.shape[0], strip_rows, padded.shape[2]), jnp.float32)
    for offset in range(tap_count):
        row_pass = row_pass + kernels[:, offset, None, None] * padded[
            :, offset : offset + strip_rows, :
        ].astype(jnp.float32)
    columns = padded.shape[2]
    widened = jnp.pad(row_pass, ((0, 0), (0, 0), (half_taps, half_taps)))
    col_pass = jnp.zeros(row_pass.shape, jnp.float32)
    for offset in range(tap_count):
        col_pass = (
            col_pass + kernels[:, offset, None, None] * widened[:, :, offset : offset + columns]
        )
    return col_pass.astype(jnp.bfloat16)


def orthonormal(images):
    gram_matrix = jnp.dot(images.T, images, precision=lax.Precision.HIGHEST)
    factor = jnp.linalg.cholesky(gram_matrix)
    return lax.linalg.triangular_solve(
        factor, images, left_side=False, lower=True, transpose_a=True
    )


def local_covariance(tile_data):
    return lax.dot_general(
        tile_data, tile_data, (((1,), (1,)), ((), ())), preferred_element_type=jnp.float32
    )


def body(sky_maps, beam_index, beam_taps, start_seed):
    channels, strip_rows, columns = sky_maps.shape
    beam_count, tap_count = beam_taps.shape
    half_taps = (tap_count - 1) // 2
    onehot = (beam_index[:, None] == jnp.arange(beam_count, dtype=jnp.int32)[None, :]).astype(
        jnp.float32
    )
    tap_rows = jnp.dot(onehot, beam_taps, precision=lax.Precision.HIGHEST)
    kernels = tap_rows / jnp.sum(tap_rows, axis=1, keepdims=True)
    padded = with_halo(sky_maps, (("sky", 1),), half_taps)
    smoothed = column_pass(padded, kernels, strip_rows, half_taps, tap_count)
    freq_count = lax.axis_size("freq")
    sky_count = lax.axis_size("sky")
    tile_cols = columns // freq_count
    grouped = lax.all_to_all(
        smoothed.reshape(channels, strip_rows, freq_count, tile_cols),
        "freq",
        split_axis=2,
        concat_axis=0,
        tiled=True,
    )
    all_chans = channels * freq_count
    tile_data = grouped.reshape(all_chans, strip_rows * tile_cols)
    wide_tile = tile_data.astype(jnp.float32)
    total_pixels = strip_rows * columns * sky_count
    subspace = start_seed.astype(jnp.float32)
    covariance = lax.psum(local_covariance(tile_data), ("freq", "sky")) / total_pixels
    for sweep in range(ITERS):
        images = jnp.dot(covariance, subspace, precision=lax.Precision.HIGHEST)
        subspace = orthonormal(images)
    coeffs = jnp.dot(subspace.T, wide_tile, precision=lax.Precision.HIGHEST)
    cleaned = (wide_tile - jnp.dot(subspace, coeffs, precision=lax.Precision.HIGHEST)).astype(
        jnp.bfloat16
    )
    return cleaned.reshape(all_chans, 1, strip_rows * tile_cols)


def solution(mesh):
    return jax.shard_map(
        body,
        mesh=mesh,
        in_specs=(P("freq", "sky", None), P("freq"), P(), P()),
        out_specs=P(None, ("freq", "sky"), None),
        check_vma=False,
    )
```

profile of v0, /device:TPU:2, one launch (start us, length us, event | category | flops | bytes accessed | tf_op | source)
XLA Modules:
  0.0 664.6 jit_solution(16235698417459183960)
XLA Ops:
  6.5 2.9 fusion.109
  9.5 1.2 copy.36
  10.7 3.4 collective-permute-start
  14.1 1.2 copy.37
  15.2 2.6 collective-permute-start.1
  18.6 0.5 slice_reduce_fusion.30
  19.4 37.7 %collective-permute-done = bf16[16,15,4096]{2,0,1:T(8,128)(2,1)S(1)} collective-permute-done((bf16[16,15,4096]{2,0,1:T(8,128)(2,1)S(1)}, bf16[16,15,4096]{2,0,1:T(8,128)(2,1)S(1)}, u32[]{:S(2)}, u32[]{:S(2)}) %collective-permute-start) | collective-permute-done | bytes 1966112 | tf_op jit(solution)/shard_map/ppermute | solution.py:16
  57.1 1.1 copy.24
  58.2 3.2 collective-permute-done.1
  61.4 1.1 copy_dynamic-update-slice_fusion
  62.5 40.9 %multiply_add_fusion = f32[16,24,4096]{2,1,0:T(8,128)S(1)} fusion(bf16[16,24,4096]{2,1,0:T(8,128)(2,1)S(1)} %copy-done.2, bf16[16,15,4096]{2,1,0:T(8,128)(2,1)S(1)} %copy.24, bf16[16,39,4096]{2,1,0:T(8,128)(2,1)S(1)} %copy_dynamic-update-slice_fusion, f32[16]{0:T(128)S(1)} %get-tuple-element.8, f32[16]{0:T(128)S(1)} %get-tuple-element.9, ...), kind=kLoop, calls=%fused_computation.62 | loop fusion | flops 215482368 | bytes 58591168 | tf_op jit(solution)/shard_map/add | solution.py:25
  103.4 50.4 %add_convert_fusion = bf16[16,24,4096]{2,1,0:T(8,128)(2,1)S(1)} fusion(f32[16,24,4096]{2,1,0:T(8,128)S(1)} %multiply_add_fusion, f32[16]{0:T(128)S(1)} %get-tuple-element.8, f32[16]{0:T(128)S(1)} %get-tuple-element.9, f32[16]{0:T(128)S(1)} %get-tuple-element.10, f32[16]{0:T(128)S(1)} %get-tuple-element.11, f32[16]{0:T(128)S(1)} %get-tuple-element.12, ...), kind=kLoop, calls=%fused_computation.29 | loop fusion | flops 97517568 | bytes 9439168 | tf_op jit(solution)/shard_map/convert_element_type | solution.py:35
  153.8 7.9 %reshape.54 = bf16[16,24,64,64]{3,2,1,0:T(8,128)(2,1)} reshape(bf16[16,24,4096]{2,1,0:T(8,128)(2,1)S(1)} %add_convert_fusion) | data formatting | bytes 6291456 | tf_op jit(solution)/shard_map/reshape | solution.py:67
  161.7 9.5 %copy.40 = bf16[16,24,64,64]{3,1,0,2:T(8,128)(2,1)} copy(bf16[16,24,64,64]{3,2,1,0:T(8,128)(2,1)} %reshape.54) | data formatting | bytes 6291456 | tf_op jit(solution)/shard_map/reshape | solution.py:67
  171.2 9.7 %reshape.118 = bf16[64,2,12288]{2,1,0:T(2,128)(2,1)S(1)} reshape(bf16[64,16,24,64]{3,2,1,0:T(8,128)(2,1)} %bitcast.141) | data formatting | bytes 6291456
  180.9 85.0 %all_to_all.15 = bf16[64,2,12288]{2,1,0:T(2,128)(2,1)} all-to-all(bf16[64,2,12288]{2,1,0:T(2,128)(2,1)S(1)} %reshape.118), channel_id=1, replica_groups=mesh['freq'=64,'sky'=4] {'freq'}, dimensions={0} | all-to-all | bytes 6291456 | tf_op jit(solution)/shard_map/all_to_all | solution.py:66
  265.9 11.1 %reshape.119 = bf16[64,16,24,64]{3,2,1,0:T(8,128)(2,1)} reshape(bf16[64,2,12288]{2,1,0:T(2,128)(2,1)} %all_to_all.15) | data formatting | bytes 6291456
  277.0 7.4 %bitcast_bitcast_fusion = bf16[64,16,24,1,64]{4,2,1,0,3:T(8,128)(2,1)} fusion(bf16[64,16,24,64]{3,2,1,0:T(8,128)(2,1)} %reshape.119), kind=kLoop, calls=%fused_computation.224 | loop fusion | bytes 6291456 | tf_op jit(solution)/shard_map/all_to_all | solution.py:66
  284.5 7.9 %reshape.55 = bf16[1024,1536]{1,0:T(8,128)(2,1)S(1)} reshape(bf16[64,16,24,1,64]{4,2,1,0,3:T(8,128)(2,1)} %bitcast_bitcast_fusion) | data formatting | bytes 6291456 | tf_op jit(solution)/shard_map/reshape | solution.py:74
  292.4 5.4 fusion.111
  297.8 267.5 %all-reduce.3.cloned.1.call-done = f32[1024,1024]{1,0:T(8,128)} async-done(((f32[1024,1024]{1,0:T(8,128)}), f32[1024,1024]{1,0:T(8,128)}) %all-reduce.3.cloned.1.call-update) | async-done | bytes 4194320 | tf_op jit(solution)/shard_map/psum | solution.py:78
  565.3 5.9 fusion.50
  571.5 1.5 cholesky.134
  573.0 0.6 compare_reduce_fusion.7
  573.7 0.6 fusion.61
  574.3 1.2 custom-call.12
  575.8 5.9 fusion.48
  582.0 1.5 cholesky.145
  583.5 0.6 compare_reduce_fusion.6
  584.1 0.6 fusion.62
  584.8 1.2 custom-call.13
  586.3 5.9 fusion.46
  592.5 1.5 cholesky.156
  594.0 0.6 compare_reduce_fusion.5
  594.6 0.6 fusion.63
  595.3 1.2 custom-call.14
  596.8 5.9 fusion.44
  602.9 1.6 cholesky.167
  604.6 0.6 compare_reduce_fusion.4
  605.3 0.6 fusion.64
  605.9 1.2 custom-call.15
  607.4 5.9 fusion.42
  613.6 1.5 cholesky.178
  615.1 0.6 compare_reduce_fusion.3
  615.7 0.6 fusion.65
  616.4 1.2 custom-call.16
  617.9 5.9 fusion.40
  624.1 1.5 cholesky.189
  625.6 0.6 compare_reduce_fusion.2
  626.2 0.6 fusion.66
  626.9 1.2 custom-call.17
  628.4 5.9 fusion.38
  634.5 1.5 cholesky.200
  636.1 0.6 compare_reduce_fusion.1
  636.7 0.6 fusion.67
  637.4 1.2 custom-call.18
  638.9 5.9 fusion.36
  644.7 0.4 fusion.119
  645.2 1.5 cholesky.211
  646.8 0.6 compare_reduce_fusion
  647.4 0.6 fusion.68
  648.1 1.2 custom-call.19
  649.6 1.3 fusion.120
  650.9 6.7 %fusion.21 = bf16[1024,1,1536]{2,0,1:T(8,128)(2,1)} fusion(f32[1024,16]{0,1:T(8,128)S(1)} %convolution_bitcast_fusion, f32[16,1536]{1,0:T(8,128)S(1)} %fusion.120, bf16[1024,1536]{1,0:T(8,128)(2,1)S(1)} %reshape.55), kind=kOutput, calls=%fused_computation.63 | convolution fusion | flops 306708480 | bytes 6455296 | tf_op jit(solution)/shard_map/dot_general | solution.py:83
  (55 shorter events, 5.6 us)
Async XLA Ops:
  6.5 11.3 %copy-start = (f32[8,31]{1,0:T(8,128)S(1)}, f32[8,31]{1,0:T(8,128)}, u32[]{:S(2)}) copy-start(f32[8,31]{1,0:T(8,128)} %param.9) | copy-start | bytes 2980
  6.5 11.3 %copy-start.4 = (s32[16]{0:T(128)S(1)}, s32[16]{0:T(128)}, u32[]{:S(2)}) copy-start(s32[16]{0:T(128)} %param.8) | copy-start | bytes 196
  6.5 558.8 %all-reduce.3.cloned.1.call-start = ((), (), s32[]{:S(2)}) async-start(), calls=%async_computation.1 | async-start | bytes 8388608 | tf_op jit(solution)/shard_map/psum | solution.py:78
  9.5 9.6 %copy-start.2 = (bf16[16,24,4096]{2,1,0:T(8,128)(2,1)S(1)}, bf16[16,24,4096]{2,1,0:T(8,128)(2,1)}, u32[]{:S(2)}) copy-start(bf16[16,24,4096]{2,1,0:T(8,128)(2,1)} %param.7) | copy-start | bytes 9437188
  10.7 46.5 %collective-permute-start = (bf16[16,15,4096]{2,0,1:T(8,128)(2,1)S(1)}, bf16[16,15,4096]{2,0,1:T(8,128)(2,1)S(1)}, u32[]{:S(2)}, u32[]{:S(2)}) collective-permute-start(bf16[16,15,4096]{2,0,1:T(8,128)(2,1)S(1)} %copy.36), channel_id=1, source_target_pairs={{0,1},{1,2},{2,3},{4,5},{5,6},{6,7},{8,9},{9,10},{10,11},{12,13},{... | collective-permute-start | bytes 5898248 | tf_op jit(solution)/shard_map/ppermute | solution.py:16
  15.2 46.2 %collective-permute-start.1 = (bf16[16,15,4096]{2,0,1:T(8,128)(2,1)S(1)}, bf16[16,15,4096]{2,0,1:T(8,128)(2,1)S(1)}, u32[]{:S(2)}, u32[]{:S(2)}) collective-permute-start(bf16[16,15,4096]{2,0,1:T(8,128)(2,1)S(1)} %copy.37), channel_id=1, source_target_pairs={{1,0},{2,1},{3,2},{5,4},{6,5},{7,6},{9,8},{10,9},{11,10},{13,12},{... | collective-permute-start | bytes 5898248 | tf_op jit(solution)/shard_map/ppermute | solution.py:17
  292.4 273.0 %copy-start.3 = (s32[1024,16]{0,1:T(8,128)S(1)}, s32[1024,16]{0,1:T(8,128)}, u32[]{:S(2)}) copy-start(s32[1024,16]{0,1:T(8,128)} %param.10) | copy-start | bytes 196612
  638.6 18.9 %copy-start.1 = (f32[8,31]{1,0:T(8,128)S(1)}, f32[8,31]{1,0:T(8,128)}, u32[]{:S(2)}) copy-start(f32[8,31]{1,0:T(8,128)} %param.9) | copy-start | bytes 2980
Sparse Core Ops, SparseCore 0:
  297.9 267.3 all-reduce.2
where the time goes:
time: 671 us; the launch traced here: 665 us
  waiting for transfers between devices  308 us (46%)
  other arithmetic  124 us (18%)
  blocking collectives  85 us (13%)
  matrix products  64.5 us (10%)
  local copies, waits for them, and re-layouts  62.9 us (9%)
  between operations  13.9 us (2%)
    psum x1, waiting for transfers between devices, body(): lax.psum(local_covariance(tile_data), ('freq', 'sky')) / total_pixels  268 us
    all_to_all x1, blocking collectives, body(): lax.all_to_all(smoothed.reshape(channels, strip_rows, freq_count, tile_co...  85 us
    convert_element_type x1, other arithmetic, column_pass(): return col_pass.astype(jnp.bfloat16)  50.4 us
    dot_general x8, matrix products, body(): images = jnp.dot(covariance, subspace, precision=lax.Precision.HIGHEST)  47 us
    add x1, other arithmetic, column_pass(): row_pass + kernels[:, offset, None, None] * padded[:, offset:offset + str...  40.9 us
    ppermute x1, waiting for transfers between devices, with_halo(): before = lax.ppermute(last, axis, up)  37.7 us
    unnamed x15, local copies, waits for them, and re-layouts  23.5 us
    another operation x24, other arithmetic, orthonormal(): factor = jnp.linalg.cholesky(gram_matrix)  17.5 us
  transfers between devices with their start and end apart: 3, of which 3 were waited for; matrix products, arithmetic and copies ran while one was open for 1% of the time, Pallas kernels for 0%

commit v1 on v0

--- a/solution.py
+++ b/solution.py
@@ -75,7 +75,7 @@
     wide_tile = tile_data.astype(jnp.float32)
     total_pixels = strip_rows * columns * sky_count
     subspace = start_seed.astype(jnp.float32)
-    covariance = lax.psum(local_covariance(tile_data), ("freq", "sky")) / total_pixels
+    covariance = lax.psum(lax.psum(local_covariance(tile_data), "freq"), "sky") / total_pixels
     for sweep in range(ITERS):
         images = jnp.dot(covariance, subspace, precision=lax.Precision.HIGHEST)
         subspace = orthonormal(images)

time: 671 us -> 696 us (1.037)
  waiting for transfers between devices: 308 us -> 332 us
    psum x1 -> x2, waiting for transfers between devices: 268 us -> 291 us  [the longest x1 193 us: body(): lax.psum(local_covariance(tile_data), 'freq')]
  transfers between devices with their start and end apart: 3 -> 4, of which waited for: 3 -> 4; matrix products, arithmetic and copies ran while one was open for 1% -> 1% of each run, Pallas kernels for 0% -> 0%
where the time goes in v1:
time: 696 us; the launch traced here: 688 us
  waiting for transfers between devices  332 us (48%)
  other arithmetic  124 us (18%)
  blocking collectives  85 us (12%)
  matrix products  64.1 us (9%)
  local copies, waits for them, and re-layouts  62.9 us (9%)
  between operations  13.9 us (2%)
    psum x1, waiting for transfers between devices, body(): lax.psum(local_covariance(tile_data), 'freq')  193 us
    psum x1, waiting for transfers between devices, body(): lax.psum(lax.psum(local_covariance(tile_data), 'freq'), 'sky')  97.9 us
    all_to_all x1, blocking collectives, body(): lax.all_to_all(smoothed.reshape(channels, strip_rows, freq_count, tile_co...  85 us
    convert_element_type x1, other arithmetic, column_pass(): return col_pass.astype(jnp.bfloat16)  50.4 us
    dot_general x8, matrix products, body(): images = jnp.dot(covariance, subspace, precision=lax.Precision.HIGHEST)  47.2 us
    add x1, other arithmetic, column_pass(): row_pass + kernels[:, offset, None, None] * padded[:, offset:offset + str...  40.9 us
    ppermute x1, waiting for transfers between devices, with_halo(): before = lax.ppermute(last, axis, up)  37.7 us
    unnamed x15, local copies, waits for them, and re-layouts  23.5 us
  transfers between devices with their start and end apart: 4, of which 4 were waited for; matrix products, arithmetic and copies ran while one was open for 1% of the time, Pallas kernels for 0%

profile of v1, /device:TPU:2, one launch (start us, length us, event | category | flops | bytes accessed | tf_op | source)
XLA Modules:
  0.0 688.2 jit_solution(17326800613658973548)
XLA Ops:
  6.5 2.9 fusion.109
  9.5 1.2 copy.36
  10.7 3.4 collective-permute-start
  14.1 1.2 copy.37
  15.2 2.6 collective-permute-start.1
  18.6 0.5 slice_reduce_fusion.30
  19.4 37.7 %collective-permute-done = bf16[16,15,4096]{2,0,1:T(8,128)(2,1)S(1)} collective-permute-done((bf16[16,15,4096]{2,0,1:T(8,128)(2,1)S(1)}, bf16[16,15,4096]{2,0,1:T(8,128)(2,1)S(1)}, u32[]{:S(2)}, u32[]{:S(2)}) %collective-permute-start) | collective-permute-done | bytes 1966112 | tf_op jit(solution)/shard_map/ppermute | solution.py:16
  57.1 1.1 copy.24
  58.2 3.2 collective-permute-done.1
  61.4 1.1 copy_dynamic-update-slice_fusion
  62.5 40.9 %multiply_add_fusion = f32[16,24,4096]{2,1,0:T(8,128)S(1)} fusion(bf16[16,24,4096]{2,1,0:T(8,128)(2,1)S(1)} %copy-done.2, bf16[16,15,4096]{2,1,0:T(8,128)(2,1)S(1)} %copy.24, bf16[16,39,4096]{2,1,0:T(8,128)(2,1)S(1)} %copy_dynamic-update-slice_fusion, f32[16]{0:T(128)S(1)} %get-tuple-element.8, f32[16]{0:T(128)S(1)} %get-tuple-element.9, ...), kind=kLoop, calls=%fused_computation.62 | loop fusion | flops 215482368 | bytes 58591168 | tf_op jit(solution)/shard_map/add | solution.py:25
  103.4 50.4 %add_convert_fusion = bf16[16,24,4096]{2,1,0:T(8,128)(2,1)S(1)} fusion(f32[16,24,4096]{2,1,0:T(8,128)S(1)} %multiply_add_fusion, f32[16]{0:T(128)S(1)} %get-tuple-element.8, f32[16]{0:T(128)S(1)} %get-tuple-element.9, f32[16]{0:T(128)S(1)} %get-tuple-element.10, f32[16]{0:T(128)S(1)} %get-tuple-element.11, f32[16]{0:T(128)S(1)} %get-tuple-element.12, ...), kind=kLoop, calls=%fused_computation.29 | loop fusion | flops 97517568 | bytes 9439168 | tf_op jit(solution)/shard_map/convert_element_type | solution.py:35
  153.8 7.9 %reshape.54 = bf16[16,24,64,64]{3,2,1,0:T(8,128)(2,1)} reshape(bf16[16,24,4096]{2,1,0:T(8,128)(2,1)S(1)} %add_convert_fusion) | data formatting | bytes 6291456 | tf_op jit(solution)/shard_map/reshape | solution.py:67
  161.7 9.5 %copy.40 = bf16[16,24,64,64]{3,1,0,2:T(8,128)(2,1)} copy(bf16[16,24,64,64]{3,2,1,0:T(8,128)(2,1)} %reshape.54) | data formatting | bytes 6291456 | tf_op jit(solution)/shard_map/reshape | solution.py:67
  171.2 9.7 %reshape.118 = bf16[64,2,12288]{2,1,0:T(2,128)(2,1)S(1)} reshape(bf16[64,16,24,64]{3,2,1,0:T(8,128)(2,1)} %bitcast.141) | data formatting | bytes 6291456
  180.9 85.0 %all_to_all.15 = bf16[64,2,12288]{2,1,0:T(2,128)(2,1)} all-to-all(bf16[64,2,12288]{2,1,0:T(2,128)(2,1)S(1)} %reshape.118), channel_id=1, replica_groups=mesh['freq'=64,'sky'=4] {'freq'}, dimensions={0} | all-to-all | bytes 6291456 | tf_op jit(solution)/shard_map/all_to_all | solution.py:66
  265.9 11.1 %reshape.119 = bf16[64,16,24,64]{3,2,1,0:T(8,128)(2,1)} reshape(bf16[64,2,12288]{2,1,0:T(2,128)(2,1)} %all_to_all.15) | data formatting | bytes 6291456
  277.0 7.4 %bitcast_bitcast_fusion = bf16[64,16,24,1,64]{4,2,1,0,3:T(8,128)(2,1)} fusion(bf16[64,16,24,64]{3,2,1,0:T(8,128)(2,1)} %reshape.119), kind=kLoop, calls=%fused_computation.224 | loop fusion | bytes 6291456 | tf_op jit(solution)/shard_map/all_to_all | solution.py:66
  284.5 7.9 %reshape.55 = bf16[1024,1536]{1,0:T(8,128)(2,1)S(1)} reshape(bf16[64,16,24,1,64]{4,2,1,0,3:T(8,128)(2,1)} %bitcast_bitcast_fusion) | data formatting | bytes 6291456 | tf_op jit(solution)/shard_map/reshape | solution.py:74
  292.4 5.0 fusion.111
  297.9 193.1 %all-reduce.4.cloned.1.call-done = f32[1024,1024]{1,0:T(8,128)} async-done(((f32[1024,1024]{1,0:T(8,128)}), f32[1024,1024]{1,0:T(8,128)}) %all-reduce.4.cloned.1.call-update) | async-done | bytes 4194320 | tf_op jit(solution)/shard_map/psum | solution.py:78
  491.1 97.9 %all-reduce.6.cloned.1.call-done = f32[1024,1024]{1,0:T(8,128)} async-done(((f32[1024,1024]{1,0:T(8,128)}), f32[1024,1024]{1,0:T(8,128)}) %all-reduce.6.cloned.1.call-update) | async-done | bytes 4194320 | tf_op jit(solution)/shard_map/psum | solution.py:78
  589.0 5.9 fusion.50
  595.1 1.5 cholesky.134
  596.7 0.6 compare_reduce_fusion.7
  597.3 0.6 fusion.61
  598.0 1.2 custom-call.12
  599.5 5.9 fusion.48
  605.6 1.5 cholesky.145
  607.1 0.6 compare_reduce_fusion.6
  607.8 0.6 fusion.62
  608.5 1.2 custom-call.13
  610.0 5.9 fusion.46
  616.1 1.5 cholesky.156
  617.6 0.6 compare_reduce_fusion.5
  618.3 0.6 fusion.63
  618.9 1.2 custom-call.14
  620.4 5.9 fusion.44
  626.6 1.6 cholesky.167
  628.3 0.6 compare_reduce_fusion.4
  628.9 0.6 fusion.64
  629.6 1.2 custom-call.15
  631.1 5.9 fusion.42
  637.2 1.5 cholesky.178
  638.7 0.6 compare_reduce_fusion.3
  639.4 0.6 fusion.65
  640.0 1.2 custom-call.16
  641.6 5.9 fusion.40
  647.7 1.5 cholesky.189
  649.2 0.6 compare_reduce_fusion.2
  649.9 0.6 fusion.66
  650.5 1.2 custom-call.17
  652.0 5.9 fusion.38
  658.2 1.5 cholesky.200
  659.7 0.6 compare_reduce_fusion.1
  660.4 0.6 fusion.67
  661.0 1.2 custom-call.18
  662.5 6.1 fusion.36
  668.9 1.5 cholesky.211
  670.4 0.6 compare_reduce_fusion
  671.0 0.6 fusion.68
  671.7 1.2 custom-call.19
  673.2 1.3 fusion.120
  674.5 6.7 fusion.21
  (58 shorter events, 6.2 us)
Async XLA Ops:
  6.5 11.3 %copy-start = (f32[8,31]{1,0:T(8,128)S(1)}, f32[8,31]{1,0:T(8,128)}, u32[]{:S(2)}) copy-start(f32[8,31]{1,0:T(8,128)} %param.9) | copy-start | bytes 2980
  6.5 11.3 %copy-start.4 = (s32[16]{0:T(128)S(1)}, s32[16]{0:T(128)}, u32[]{:S(2)}) copy-start(s32[16]{0:T(128)} %param.8) | copy-start | bytes 196
  6.5 484.5 %all-reduce.4.cloned.1.call-start = ((), (), s32[]{:S(2)}) async-start(), calls=%async_computation.1 | async-start | bytes 8388608 | tf_op jit(solution)/shard_map/psum | solution.py:78
  9.5 9.6 %copy-start.2 = (bf16[16,24,4096]{2,1,0:T(8,128)(2,1)S(1)}, bf16[16,24,4096]{2,1,0:T(8,128)(2,1)}, u32[]{:S(2)}) copy-start(bf16[16,24,4096]{2,1,0:T(8,128)(2,1)} %param.7) | copy-start | bytes 9437188
  10.7 46.5 %collective-permute-start = (bf16[16,15,4096]{2,0,1:T(8,128)(2,1)S(1)}, bf16[16,15,4096]{2,0,1:T(8,128)(2,1)S(1)}, u32[]{:S(2)}, u32[]{:S(2)}) collective-permute-start(bf16[16,15,4096]{2,0,1:T(8,128)(2,1)S(1)} %copy.36), channel_id=1, source_target_pairs={{0,1},{1,2},{2,3},{4,5},{5,6},{6,7},{8,9},{9,10},{10,11},{12,13},{... | collective-permute-start | bytes 5898248 | tf_op jit(solution)/shard_map/ppermute | solution.py:16
  15.2 46.2 %collective-permute-start.1 = (bf16[16,15,4096]{2,0,1:T(8,128)(2,1)S(1)}, bf16[16,15,4096]{2,0,1:T(8,128)(2,1)S(1)}, u32[]{:S(2)}, u32[]{:S(2)}) collective-permute-start(bf16[16,15,4096]{2,0,1:T(8,128)(2,1)S(1)} %copy.37), channel_id=1, source_target_pairs={{1,0},{2,1},{3,2},{5,4},{6,5},{7,6},{9,8},{10,9},{11,10},{13,12},{... | collective-permute-start | bytes 5898248 | tf_op jit(solution)/shard_map/ppermute | solution.py:17
  297.4 291.6 %copy-start.3 = (s32[1024,16]{0,1:T(8,128)S(1)}, s32[1024,16]{0,1:T(8,128)}, u32[]{:S(2)}) copy-start(s32[1024,16]{0,1:T(8,128)} %param.10) | copy-start | bytes 196612
  297.5 291.5 %all-reduce.6.cloned.1.call-start = ((), (), s32[]{:S(2)}) async-start(), calls=%async_computation.2 | async-start | bytes 8388608 | tf_op jit(solution)/shard_map/psum | solution.py:78
  662.2 18.9 %copy-start.1 = (f32[8,31]{1,0:T(8,128)S(1)}, f32[8,31]{1,0:T(8,128)}, u32[]{:S(2)}) copy-start(f32[8,31]{1,0:T(8,128)} %param.9) | copy-start | bytes 2980
Sparse Core Ops, SparseCore 0:
  297.6 193.4 all-reduce.3
  493.4 95.5 all-reduce.5
